TPU v7x, 512 devices: a whole 4x8x8 slice. The times are simulated.
512 devices in a mesh: rep: 16 (over y, core), tp: 32 (over z, x).
Axes of the slice: x: 4, y: 8, z: 8, core: 2. Of those that a mesh axis runs over, the one named last changes fastest.
Arguments:
- tokens: bfloat16 [8192, 8192], P('rep', 'tp'), may hold values from -6 to 6
- base_weight: bfloat16 [8192, 8192], P(None, 'tp'), may hold values from -0.0625 to 0.0625
- delta: bfloat16 [48, 64, 2, 128, 128], P('rep', 'tp'), may hold values from -0.375 to 0.375
- live_blocks: int32 [48, 64, 2], P(None, 'tp'), may hold values from 0 to 63, as said below
- row_variant: int32 [8192, 1], P('rep'), may hold values from 0 to 47; in each aligned block of 512 rows (0 to 511, 512 to 1023, ...) at most 21 rows name the same one
Outputs:
- projected: bfloat16 [8192, 8192], P('rep', 'tp')
Inputs may be any that keep to these rules, and one draw needn't show every extreme that they name: `live_blocks`: the 2 block rows listed for one variant and column block are distinct. `row_variant`: among the rows of one index of rep no variant appears more than 21 times, and some variant appears exactly 21 times.
All inputs are finite; a program needn't handle non-finite values.
Results may differ from a plain program's by a relative error of at most 0.0039.
Values may be sent and summed in bfloat16 or wider, within the bound.
A program may use at most 128 MiB of HBM per device.

v0:
```python
import jax
import jax.numpy as jnp
from jax import lax
from jax.sharding import PartitionSpec as P


def multiply(received, weight_tables):
    sources, local_variants, slot_count, feat_width = received.shape
    col_blocks = weight_tables.shape[1]
    block_size = weight_tables.shape[3]
    shaped = received.reshape(
        sources, local_variants, slot_count, col_blocks, feat_width // col_blocks
    )
    flat_weights = weight_tables.reshape(
        local_variants, col_blocks, feat_width // col_blocks, block_size
    )
    result = jnp.einsum(
        "auncf,ucfb->auncb", shaped, flat_weights, preferred_element_type=jnp.float32
    )
    return result.astype(jnp.bfloat16).reshape(
        sources, local_variants, slot_count, col_blocks * block_size
    )


def local(tokens, base_weight, delta, live_blocks, row_variant):
    rep_count = lax.axis_size("rep")
    local_variants = delta.shape[0]
    col_blocks = delta.shape[1]
    live_count = delta.shape[2]
    block_size = delta.shape[3]
    variants = local_variants * rep_count
    row_count = tokens.shape[0]
    capacity = max(2, 2 * row_count // variants)
    feat_width = col_blocks * live_count * block_size
    features_all = lax.all_gather(tokens, "tp", axis=1, tiled=True)
    base_part = jnp.dot(features_all, base_weight, preferred_element_type=jnp.float32)
    variant = row_variant[:, 0]
    onehot = (variant[:, None] == jnp.arange(variants, dtype=jnp.int32)[None, :]).astype(jnp.int32)
    row_rank = jnp.sum((jnp.cumsum(onehot, axis=0) - 1) * onehot, axis=1)
    slot_index = variant * capacity + row_rank
    tile_indices = jnp.take(live_blocks, variant, axis=0).reshape(
        row_count, col_blocks * live_count
    )
    blocks_view = features_all.reshape(row_count, features_all.shape[1] // block_size, block_size)
    picked = jnp.take_along_axis(blocks_view, tile_indices[:, :, None], axis=1).reshape(
        row_count, feat_width
    )
    outgoing = jnp.zeros((variants * capacity, feat_width), jnp.bfloat16).at[slot_index].set(picked)
    all_deltas = lax.all_gather(delta, "rep", axis=0, tiled=True)
    returned = multiply(outgoing.reshape(1, variants, capacity, feat_width), all_deltas)
    returned_flat = returned.reshape(variants * capacity, col_blocks * block_size)
    correction_summand = jnp.take(returned_flat, slot_index, axis=0)
    return (base_part + correction_summand.astype(jnp.float32)).astype(jnp.bfloat16)


def solution(mesh):
    placed = (
        P("rep", "tp"),
        P(None, "tp"),
        P("rep", "tp", None, None, None),
        P(None, "tp", None),
        P("rep", None),
    )
    return jax.shard_map(
        local, mesh=mesh, in_specs=placed, out_specs=P("rep", "tp"), check_vma=False
    )
```

profile of v0, /device:TPU:1, one launch (start us, length us, event | category | flops | bytes accessed | tf_op | source)
XLA Modules:
  0.0 194.5 jit_solution(5336732794186079991)
XLA Ops:
  6.5 0.7 all-gather.3.cloned.1.call-update
  7.3 0.7 all-gather.5.cloned.1.call-update
  8.0 0.7 fusion.9
  8.7 1.2 reduce-window.6
  9.9 0.2 slice_reduce_fusion
  10.2 0.8 copy.20
  11.0 0.8 fusion.8
  11.7 0.7 and_reduce_fusion
  12.5 2.1 %gather_fusion = s32[512,2,2]{2,1,0:T(2,128)S(1)} fusion(s32[48,2,2]{2,1,0:T(2,128)S(1)} %copy.20, s32[1024]{0:T(1024)S(1)} %pad_clamp_fusion.1), kind=kCustom, calls=%fused_computation | custom fusion | bytes 18432 | tf_op jit(solution)/shard_map/jit(_take)/gather | solution.py:41
  14.6 0.2 copy.21
  14.8 0.1 copy.24
  15.0 0.2 reshape.171
  15.2 0.2 copy.22
  15.4 105.8 %all-gather.3.cloned.1.call-done = bf16[512,8192]{1,0:T(8,128)(2,1)} async-done(((bf16[512,256]{1,0:T(8,128)(2,1)}), bf16[512,8192]{1,0:T(8,128)(2,1)}) %all-gather.3.cloned.1.call-update) | async-done | bytes 8388624 | tf_op jit(solution)/shard_map/all_gather | solution.py:35
  121.1 9.3 %copy.28 = bf16[64,8,64,128]{3,2,1,0:T(8,128)(2,1)} copy(bf16[64,8,64,128]{3,1,2,0:T(8,128)(2,1)} %bitcast.50) | data formatting | bytes 16777216
  130.4 24.3 %gather_fusion.2 = bf16[2048,128]{1,0:T(8,128)(2,1)S(1)} fusion(bf16[512,64,128]{2,1,0:T(8,128)(2,1)} %bitcast.48, s32[2048]{0:T(1024)S(1)} %reshape.171), kind=kCustom, calls=%fused_computation.2 | custom fusion | bytes 1064960 | tf_op jit(solution)/shard_map/jit(take_along_axis)/gather | solution.py:45
  154.8 1.6 broadcast_select_fusion
  156.4 2.7 %scatter_custom_fusion = bf16[1008,512]{1,0:T(8,128)(2,1)S(1)} fusion(s32[512]{0:T(512)S(1)} %bitcast.58, bf16[64,8,4,128]{3,2,1,0:T(4,128)(2,1)S(1)} %bitcast.52, bf16[]{:T(256)} %constant.50.clone.1), kind=kCustom, calls=%fused_computation.9 | custom fusion | bytes 1556482 | tf_op jit(solution)/shard_map/scatter | solution.py:48
  159.1 0.2 reshape.153
  159.4 14.4 %all-gather.5.cloned.1.call-done = bf16[48,2,2,128,128]{4,3,2,1,0:T(8,128)(2,1)} async-done(((bf16[3,2,2,128,128]{4,3,2,1,0:T(8,128)(2,1)}), bf16[48,2,2,128,128]{4,3,2,1,0:T(8,128)(2,1)}) %all-gather.5.cloned.1.call-update) | async-done | bytes 6291472 | tf_op jit(solution)/shard_map/all_gather | solution.py:49
  173.8 3.8 %fusion = bf16[1,48,21,2,128]{4,2,3,1,0:T(8,128)(2,1)S(1)} fusion(bf16[48,2,256,128]{3,2,1,0:T(8,128)(2,1)} %bitcast.51, bf16[48,21,2,256]{3,2,1,0:T(2,128)(2,1)S(1)} %reshape.153), kind=kOutput, calls=%fused_computation.5 | convolution fusion | flops 132378624 | bytes 7839744 | tf_op jit(solution)/shard_map/auncf,ucfb->auncb/dot_general | solution.py:17
  177.6 0.4 copy.26
  178.1 2.0 %gather_fusion.1 = bf16[512,256]{1,0:T(8,128)(2,1)S(1)} fusion(bf16[1008,256]{1,0:T(8,128)(2,1)S(1)} %bitcast.49, s32[1024]{0:T(1024)S(1)} %pad_clamp_fusion), kind=kCustom, calls=%fused_computation.1 | custom fusion | bytes 526336 | tf_op jit(solution)/shard_map/jit(_take)/gather | solution.py:52
  180.1 7.6 %fusion.1 = bf16[512,256]{1,0:T(8,128)(2,1)} fusion(bf16[512,8192]{1,0:T(8,128)(2,1)} %all-gather.3.cloned.1.call-done, bf16[8192,256]{1,0:T(8,128)(2,1)} %param.6, bf16[512,256]{1,0:T(8,128)(2,1)S(1)} %gather_fusion.1, pred[512]{0:T(512)(128)(4,1)S(1)} %get-tuple-element.9), kind=kOutput, calls=%fused_computation.7 | convolution fusion | flops 2148007936 | bytes 13107712 | tf_op jit(solution)/shard_map/dot_general | solution.py:36
  (11 shorter events, 0.2 us)
Async XLA Ops:
  6.5 114.6 %all-gather.3.cloned.1.call-start = ((), (), s32[]{:S(2)}) async-start(), calls=%async_computation | async-start | bytes 8650752 | tf_op jit(solution)/shard_map/all_gather | solution.py:35
  7.3 166.5 %all-gather.5.cloned.1.call-start = ((), (), s32[]{:S(2)}) async-start(), calls=%async_computation.1 | async-start | bytes 6684672 | tf_op jit(solution)/shard_map/all_gather | solution.py:49
Sparse Core Ops, SparseCore 0:
  10.4 110.7 all-gather.2
  123.3 50.4 all-gather.4
where the time goes:
time: 195 us
  waiting for transfers between devices  122 us (63%)
  local copies, waits for them, and re-layouts  42.9 us (22%)
  between operations  13.5 us (7%)
  matrix products  11.4 us (6%)
  other arithmetic  5.09 us (3%)
    all_gather x1, waiting for transfers between devices, local(): features_all = lax.all_gather(tokens, 'tp', axis=1, tiled=True)  106 us
    gather x3, local copies, waits for them, and re-layouts, local(): jnp.take_along_axis(blocks_view, tile_indices[:, :, None], axis=1)  24.6 us
    all_gather x1, waiting for transfers between devices, local(): all_deltas = lax.all_gather(delta, 'rep', axis=0, tiled=True)  14.4 us
    unnamed x3, local copies, waits for them, and re-layouts  10.2 us
    dot_general x1, matrix products, local(): jnp.dot(features_all, base_weight, preferred_element_type=jnp.float32)  7.61 us
  transfers between devices with their start and end apart: 2, of which 2 were waited for; matrix products, arithmetic and copies ran while one was open for 23% of the time, Pallas kernels for 0%

commit v1 on v0

--- a/solution.py
+++ b/solution.py
@@ -46,7 +46,16 @@
         row_count, feat_width
     )
     outgoing = jnp.zeros((variants * capacity, feat_width), jnp.bfloat16).at[slot_index].set(picked)
-    all_deltas = lax.all_gather(delta, "rep", axis=0, tiled=True)
+    ways = lax.axis_size("rep")
+    up = [(d, (d + 1) % ways) for d in range(ways)]
+    down = [(d, (d - 1) % ways) for d in range(ways)]
+    earlier, later = ([delta], [delta])
+    for _ in range(ways // 2):
+        earlier.append(lax.ppermute(earlier[-1], "rep", up))
+    for _ in range((ways - 1) // 2):
+        later.append(lax.ppermute(later[-1], "rep", down))
+    line = jnp.concatenate([*earlier[::-1], *later[1:]], axis=0)
+    all_deltas = jnp.roll(line, (lax.axis_index("rep") - ways // 2) * delta.shape[0], axis=0)
     returned = multiply(outgoing.reshape(1, variants, capacity, feat_width), all_deltas)
     returned_flat = returned.reshape(variants * capacity, col_blocks * block_size)
     correction_summand = jnp.take(returned_flat, slot_index, axis=0)

time: 195 us -> 183 us (0.938); the launches traced: 195 us -> 180 us
  waiting for transfers between devices: 122 us -> 31.1 us
  starting transfers between devices: 0.04 us -> 47.8 us
  local copies, waits for them, and re-layouts: 42.9 us -> 68 us
  other arithmetic: 5.09 us -> 8.26 us
    all_gather x1, waiting for transfers between devices: 106 us -> 20.2 us  [local(): features_all = lax.all_gather(tokens, 'tp', axis=1, tiled=True)]
    ppermute x0 -> x15, starting transfers between devices: none -> 47.8 us  [the longest x7 42.6 us: local(): later.append(lax.ppermute(later[-1], 'rep', down))]
    unnamed x3 -> x48, local copies, waits for them, and re-layouts: 10.2 us -> 27.5 us
    all_gather x1 -> x0, waiting for transfers between devices: 14.4 us -> none  [local(): all_deltas = lax.all_gather(delta, 'rep', axis=0, tiled=True)]
    ppermute x0 -> x15, waiting for transfers between devices: none -> 10.1 us  [the longest x8 9.46 us: local(): earlier.append(lax.ppermute(earlier[-1], 'rep', up))]
    dynamic_slice x0 -> x1, local copies, waits for them, and re-layouts: none -> 4.02 us  [local(): jnp.roll(line, (lax.axis_index('rep') - ways // 2) * delta.shape[0], axis=0)]
  transfers between devices with their start and end apart: 2 -> 16, of which waited for: 2 -> 9; matrix products, arithmetic and copies ran while one was open for 23% -> 19% of each run, Pallas kernels for 0% -> 0%
where the time goes in v1:
time: 183 us; the launch traced here: 180 us
  local copies, waits for them, and re-layouts  68 us (37%)
  starting transfers between devices  47.8 us (26%)
  waiting for transfers between devices  31.1 us (17%)
  between operations  13.8 us (8%)
  matrix products  11.3 us (6%)
  other arithmetic  8.26 us (5%)
    ppermute x7, starting transfers between devices, local(): later.append(lax.ppermute(later[-1], 'rep', down))  42.6 us
    unnamed x48, local copies, waits for them, and re-layouts  27.5 us
    gather x3, local copies, waits for them, and re-layouts, local(): jnp.take_along_axis(blocks_view, tile_indices[:, :, None], axis=1)  26.4 us
    all_gather x1, waiting for transfers between devices, local(): features_all = lax.all_gather(tokens, 'tp', axis=1, tiled=True)  20.2 us
    ppermute x8, waiting for transfers between devices, local(): earlier.append(lax.ppermute(earlier[-1], 'rep', up))  9.46 us
    dot_general x1, matrix products, local(): jnp.dot(features_all, base_weight, preferred_element_type=jnp.float32)  7.61 us
    ppermute x8, starting transfers between devices, local(): earlier.append(lax.ppermute(earlier[-1], 'rep', up))  5.13 us
    dynamic_slice x1, local copies, waits for them, and re-layouts, local(): jnp.roll(line, (lax.axis_index('rep') - ways // 2) * delta.shape[0], axis=0)  4.02 us
  transfers between devices with their start and end apart: 16, of which 9 were waited for; matrix products, arithmetic and copies ran while one was open for 19% of the time, Pallas kernels for 0%

profile of v1, /device:TPU:1, one launch (start us, length us, event | category | flops | bytes accessed | tf_op | source)
XLA Modules:
  0.0 180.3 jit_solution(5013681493526616915)
XLA Ops:
  7.3 2.7 %collective-permute-start = (bf16[3,2,2,128,128]{4,3,2,1,0:T(8,128)(2,1)}, bf16[3,2,2,128,128]{4,3,2,1,0:T(8,128)(2,1)S(1)}, u32[]{:S(2)}, u32[]{:S(2)}) collective-permute-start(bf16[3,2,2,128,128]{4,3,2,1,0:T(8,128)(2,1)} %param.7), channel_id=1, source_target_pairs={{0,32},{32,64},{64,96},{96,128},{128,160},{160,192},{192,224},{224... | collective-permute-start | bytes 1179656 | tf_op jit(solution)/shard_map/ppermute | solution.py:54
  9.9 5.6 %collective-permute-done = bf16[3,2,2,128,128]{4,3,2,1,0:T(8,128)(2,1)S(1)} collective-permute-done((bf16[3,2,2,128,128]{4,3,2,1,0:T(8,128)(2,1)}, bf16[3,2,2,128,128]{4,3,2,1,0:T(8,128)(2,1)S(1)}, u32[]{:S(2)}, u32[]{:S(2)}) %collective-permute-start) | collective-permute-done | bytes 393248 | tf_op jit(solution)/shard_map/ppermute | solution.py:54
  15.5 1.8 %collective-permute-start.1 = (bf16[3,2,2,128,128]{4,3,2,1,0:T(8,128)(2,1)S(1)}, bf16[3,2,2,128,128]{4,3,2,1,0:T(8,128)(2,1)S(1)}, u32[]{:S(2)}, u32[]{:S(2)}) collective-permute-start(bf16[3,2,2,128,128]{4,3,2,1,0:T(8,128)(2,1)S(1)} %collective-permute-done), channel_id=1, source_target_pairs={{0,32},{32,64},{64,96},{96,128},{128,160},{160,192},{192,224},{224... | collective-permute-start | bytes 1179656 | tf_op jit(solution)/shard_map/ppermute | solution.py:54
  17.4 5.4 %collective-permute-start.8 = (bf16[3,2,2,128,128]{4,3,2,1,0:T(8,128)(2,1)}, bf16[3,2,2,128,128]{4,3,2,1,0:T(8,128)(2,1)S(1)}, u32[]{:S(2)}, u32[]{:S(2)}) collective-permute-start(bf16[3,2,2,128,128]{4,3,2,1,0:T(8,128)(2,1)} %param.7), channel_id=1, source_target_pairs={{0,480},{32,0},{64,32},{96,64},{128,96},{160,128},{192,160},{224,1... | collective-permute-start | bytes 1179656 | tf_op jit(solution)/shard_map/ppermute | solution.py:56
  22.7 1.2 collective-permute-done.1
  24.8 6.5 %collective-permute-start.9 = (bf16[3,2,2,128,128]{4,3,2,1,0:T(8,128)(2,1)S(1)}, bf16[3,2,2,128,128]{4,3,2,1,0:T(8,128)(2,1)S(1)}, u32[]{:S(2)}, u32[]{:S(2)}) collective-permute-start(bf16[3,2,2,128,128]{4,3,2,1,0:T(8,128)(2,1)S(1)} %collective-permute-done.8), channel_id=1, source_target_pairs={{0,480},{32,0},{64,32},{96,64},{128,96},{160,128},{192,160},{224,1... | collective-permute-start | bytes 1179656 | tf_op jit(solution)/shard_map/ppermute | solution.py:56
  32.7 7.0 %collective-permute-start.10 = (bf16[3,2,2,128,128]{4,3,2,1,0:T(8,128)(2,1)S(1)}, bf16[3,2,2,128,128]{4,3,2,1,0:T(8,128)(2,1)S(1)}, u32[]{:S(2)}, u32[]{:S(2)}) collective-permute-start(bf16[3,2,2,128,128]{4,3,2,1,0:T(8,128)(2,1)S(1)} %collective-permute-done.9), channel_id=1, source_target_pairs={{0,480},{32,0},{64,32},{96,64},{128,96},{160,128},{192,160},{224,1... | collective-permute-start | bytes 1179656 | tf_op jit(solution)/shard_map/ppermute | solution.py:56
  39.6 1.2 collective-permute-done.3
  41.6 7.2 %collective-permute-start.11 = (bf16[3,2,2,128,128]{4,3,2,1,0:T(8,128)(2,1)S(1)}, bf16[3,2,2,128,128]{4,3,2,1,0:T(8,128)(2,1)}, u32[]{:S(2)}, u32[]{:S(2)}) collective-permute-start(bf16[3,2,2,128,128]{4,3,2,1,0:T(8,128)(2,1)S(1)} %collective-permute-done.10), channel_id=1, source_target_pairs={{0,480},{32,0},{64,32},{96,64},{128,96},{160,128},{192,160},{224,1... | collective-permute-start | bytes 1179656 | tf_op jit(solution)/shard_map/ppermute | solution.py:56
  49.9 1.2 reduce-window.6
  51.4 7.2 %collective-permute-start.12 = (bf16[3,2,2,128,128]{4,3,2,1,0:T(8,128)(2,1)}, bf16[3,2,2,128,128]{4,3,2,1,0:T(8,128)(2,1)}, u32[]{:S(2)}, u32[]{:S(2)}) collective-permute-start(bf16[3,2,2,128,128]{4,3,2,1,0:T(8,128)(2,1)} %collective-permute-done.11), channel_id=1, source_target_pairs={{0,480},{32,0},{64,32},{96,64},{128,96},{160,128},{192,160},{224,1... | collective-permute-start | bytes 1179656 | tf_op jit(solution)/shard_map/ppermute | solution.py:56
  60.2 1.8 %and_reduce_fusion = (pred[512]{0:T(512)(128)(4,1)}, s32[512,1]{0,1:T(1,128)S(1)}, pred[512]{0:T(512)(128)(4,1)}, s32[512,1]{0,1:T(1,128)}) fusion(s32[512,1]{0,1:T(1,128)} %param.9, s32[512,1]{0,1:T(1,128)S(1)} %bitcast.57), kind=kLoop, calls=%fused_computation.63 | loop fusion | flops 7168 | bytes 9216 | tf_op jit(solution)/shard_map/jit(_take)/and | solution.py:41
  62.0 2.1 %gather_fusion = s32[512,2,2]{2,1,0:T(2,128)S(1)} fusion(s32[48,2,2]{2,1,0:T(2,128)S(1)} %copy.12, s32[1024]{0:T(1024)S(1)} %pad_clamp_fusion.1), kind=kCustom, calls=%fused_computation | custom fusion | bytes 18432 | tf_op jit(solution)/shard_map/jit(_take)/gather | solution.py:41
  64.9 6.3 %collective-permute-start.13 = (bf16[3,2,2,128,128]{4,3,2,1,0:T(8,128)(2,1)}, bf16[3,2,2,128,128]{4,3,2,1,0:T(8,128)(2,1)}, u32[]{:S(2)}, u32[]{:S(2)}) collective-permute-start(bf16[3,2,2,128,128]{4,3,2,1,0:T(8,128)(2,1)} %collective-permute-done.12), channel_id=1, source_target_pairs={{0,480},{32,0},{64,32},{96,64},{128,96},{160,128},{192,160},{224,1... | collective-permute-start | bytes 1179656 | tf_op jit(solution)/shard_map/ppermute | solution.py:56
  76.8 3.0 %collective-permute-start.14 = (bf16[3,2,2,128,128]{4,3,2,1,0:T(8,128)(2,1)}, bf16[3,2,2,128,128]{4,3,2,1,0:T(8,128)(2,1)S(1)}, u32[]{:S(2)}, u32[]{:S(2)}) collective-permute-start(bf16[3,2,2,128,128]{4,3,2,1,0:T(8,128)(2,1)} %collective-permute-done.13), channel_id=1, source_target_pairs={{0,480},{32,0},{64,32},{96,64},{128,96},{160,128},{192,160},{224,1... | collective-permute-start | bytes 1179656 | tf_op jit(solution)/shard_map/ppermute | solution.py:56
  96.7 4.0 %constant_dynamic-slice_fusion = bf16[48,2,2,128,128]{4,3,2,1,0:T(8,128)(2,1)} fusion(bf16[96,2,2,128,128]{4,3,2,1,0:T(8,128)(2,1)S(1)} %constant_dynamic-update-slice_fusion, s32[]{:T(128)S(6)} %select_n.81), kind=kLoop, calls=%fused_computation.67 | loop fusion | bytes 12582916 | tf_op jit(solution)/shard_map/jit(_roll_dynamic)/dynamic_slice | solution.py:58
  100.8 20.2 %all-gather.2.cloned.1.call-done = bf16[512,8192]{1,0:T(8,128)(2,1)} async-done(((bf16[512,256]{1,0:T(8,128)(2,1)}), bf16[512,8192]{1,0:T(8,128)(2,1)}) %all-gather.2.cloned.1.call-update) | async-done | bytes 8388624 | tf_op jit(solution)/shard_map/all_gather | solution.py:35
  121.0 9.3 %copy.20 = bf16[64,8,64,128]{3,2,1,0:T(8,128)(2,1)} copy(bf16[64,8,64,128]{3,1,2,0:T(8,128)(2,1)} %bitcast.49) | data formatting | bytes 16777216
  130.3 24.4 %gather_fusion.2 = bf16[2048,128]{1,0:T(8,128)(2,1)S(1)} fusion(bf16[512,64,128]{2,1,0:T(8,128)(2,1)} %bitcast.47, s32[2048]{0:T(1024)S(1)} %reshape.171), kind=kCustom, calls=%fused_computation.2 | custom fusion | bytes 1064960 | tf_op jit(solution)/shard_map/jit(take_along_axis)/gather | solution.py:45
  154.7 1.6 broadcast_select_fusion
  156.3 3.0 %scatter_custom_fusion = bf16[1008,512]{1,0:T(8,128)(2,1)S(1)} fusion(s32[512]{0:T(512)} %bitcast.56, bf16[64,8,4,128]{3,2,1,0:T(4,128)(2,1)S(1)} %bitcast.50, bf16[]{:T(256)} %constant.79.clone.1), kind=kCustom, calls=%fused_computation.9 | custom fusion | bytes 1556992 | tf_op jit(solution)/shard_map/scatter | solution.py:48
  159.6 3.7 %fusion = bf16[1,48,21,2,128]{4,2,3,1,0:T(8,128)(2,1)S(1)} fusion(bf16[48,2,256,128]{3,2,1,0:T(8,128)(2,1)} %bitcast.46, bf16[48,21,2,256]{3,2,1,0:T(2,128)(2,1)S(1)} %reshape.154), kind=kOutput, calls=%fused_computation.5 | convolution fusion | flops 132378624 | bytes 7839744 | tf_op jit(solution)/shard_map/auncf,ucfb->auncb/dot_general | solution.py:17
  163.8 2.0 %gather_fusion.1 = bf16[512,256]{1,0:T(8,128)(2,1)S(1)} fusion(bf16[1008,256]{1,0:T(8,128)(2,1)S(1)} %bitcast.48, s32[1024]{0:T(1024)S(1)} %pad_clamp_fusion), kind=kCustom, calls=%fused_computation.1 | custom fusion | bytes 526336 | tf_op jit(solution)/shard_map/jit(_take)/gather | solution.py:61
  165.8 7.6 %fusion.1 = bf16[512,256]{1,0:T(8,128)(2,1)} fusion(bf16[512,8192]{1,0:T(8,128)(2,1)} %all-gather.2.cloned.1.call-done, bf16[8192,256]{1,0:T(8,128)(2,1)} %param.6, bf16[512,256]{1,0:T(8,128)(2,1)S(1)} %gather_fusion.1, pred[512]{0:T(512)(128)(4,1)S(1)} %copy-done.6), kind=kOutput, calls=%fused_computation.7 | convolution fusion | flops 2148007936 | bytes 13107712 | tf_op jit(solution)/shard_map/dot_general | solution.py:36
  (85 shorter events, 30.4 us)
Async XLA Ops:
  6.5 86.7 %copy-start = (bf16[3,2,2,128,128]{4,3,2,1,0:T(8,128)(2,1)S(1)}, bf16[3,2,2,128,128]{4,3,2,1,0:T(8,128)(2,1)}, u32[]{:S(2)}) copy-start(bf16[3,2,2,128,128]{4,3,2,1,0:T(8,128)(2,1)} %param.7) | copy-start | bytes 1179652
  6.5 114.4 %all-gather.2.cloned.1.call-start = ((), (), s32[]{:S(2)}) async-start(), calls=%async_computation | async-start | bytes 8650752 | tf_op jit(solution)/shard_map/all_gather | solution.py:35
  7.3 8.3 %collective-permute-start = (bf16[3,2,2,128,128]{4,3,2,1,0:T(8,128)(2,1)}, bf16[3,2,2,128,128]{4,3,2,1,0:T(8,128)(2,1)S(1)}, u32[]{:S(2)}, u32[]{:S(2)}) collective-permute-start(bf16[3,2,2,128,128]{4,3,2,1,0:T(8,128)(2,1)} %param.7), channel_id=1, source_target_pairs={{0,32},{32,64},{64,96},{96,128},{128,160},{160,192},{192,224},{224... | collective-permute-start | bytes 1179656 | tf_op jit(solution)/shard_map/ppermute | solution.py:54
  15.5 8.4 %collective-permute-start.1 = (bf16[3,2,2,128,128]{4,3,2,1,0:T(8,128)(2,1)S(1)}, bf16[3,2,2,128,128]{4,3,2,1,0:T(8,128)(2,1)S(1)}, u32[]{:S(2)}, u32[]{:S(2)}) collective-permute-start(bf16[3,2,2,128,128]{4,3,2,1,0:T(8,128)(2,1)S(1)} %collective-permute-done), channel_id=1, source_target_pairs={{0,32},{32,64},{64,96},{96,128},{128,160},{160,192},{192,224},{224... | collective-permute-start | bytes 1179656 | tf_op jit(solution)/shard_map/ppermute | solution.py:54
  17.4 7.4 %collective-permute-start.8 = (bf16[3,2,2,128,128]{4,3,2,1,0:T(8,128)(2,1)}, bf16[3,2,2,128,128]{4,3,2,1,0:T(8,128)(2,1)S(1)}, u32[]{:S(2)}, u32[]{:S(2)}) collective-permute-start(bf16[3,2,2,128,128]{4,3,2,1,0:T(8,128)(2,1)} %param.7), channel_id=1, source_target_pairs={{0,480},{32,0},{64,32},{96,64},{128,96},{160,128},{192,160},{224,1... | collective-permute-start | bytes 1179656 | tf_op jit(solution)/shard_map/ppermute | solution.py:56
  23.9 8.4 %collective-permute-start.2 = (bf16[3,2,2,128,128]{4,3,2,1,0:T(8,128)(2,1)S(1)}, bf16[3,2,2,128,128]{4,3,2,1,0:T(8,128)(2,1)S(1)}, u32[]{:S(2)}, u32[]{:S(2)}) collective-permute-start(bf16[3,2,2,128,128]{4,3,2,1,0:T(8,128)(2,1)S(1)} %collective-permute-done.1), channel_id=1, source_target_pairs={{0,32},{32,64},{64,96},{96,128},{128,160},{160,192},{192,224},{224... | collective-permute-start | bytes 1179656 | tf_op jit(solution)/shard_map/ppermute | solution.py:54
  24.8 7.9 %collective-permute-start.9 = (bf16[3,2,2,128,128]{4,3,2,1,0:T(8,128)(2,1)S(1)}, bf16[3,2,2,128,128]{4,3,2,1,0:T(8,128)(2,1)S(1)}, u32[]{:S(2)}, u32[]{:S(2)}) collective-permute-start(bf16[3,2,2,128,128]{4,3,2,1,0:T(8,128)(2,1)S(1)} %collective-permute-done.8), channel_id=1, source_target_pairs={{0,480},{32,0},{64,32},{96,64},{128,96},{160,128},{192,160},{224,1... | collective-permute-start | bytes 1179656 | tf_op jit(solution)/shard_map/ppermute | solution.py:56
  32.4 8.4 %collective-permute-start.3 = (bf16[3,2,2,128,128]{4,3,2,1,0:T(8,128)(2,1)S(1)}, bf16[3,2,2,128,128]{4,3,2,1,0:T(8,128)(2,1)S(1)}, u32[]{:S(2)}, u32[]{:S(2)}) collective-permute-start(bf16[3,2,2,128,128]{4,3,2,1,0:T(8,128)(2,1)S(1)} %collective-permute-done.2), channel_id=1, source_target_pairs={{0,32},{32,64},{64,96},{96,128},{128,160},{160,192},{192,224},{224... | collective-permute-start | bytes 1179656 | tf_op jit(solution)/shard_map/ppermute | solution.py:54
  32.7 8.3 %collective-permute-start.10 = (bf16[3,2,2,128,128]{4,3,2,1,0:T(8,128)(2,1)S(1)}, bf16[3,2,2,128,128]{4,3,2,1,0:T(8,128)(2,1)S(1)}, u32[]{:S(2)}, u32[]{:S(2)}) collective-permute-start(bf16[3,2,2,128,128]{4,3,2,1,0:T(8,128)(2,1)S(1)} %collective-permute-done.9), channel_id=1, source_target_pairs={{0,480},{32,0},{64,32},{96,64},{128,96},{160,128},{192,160},{224,1... | collective-permute-start | bytes 1179656 | tf_op jit(solution)/shard_map/ppermute | solution.py:56
  40.8 0.8 copy-start.1
  40.8 8.4 %collective-permute-start.4 = (bf16[3,2,2,128,128]{4,3,2,1,0:T(8,128)(2,1)S(1)}, bf16[3,2,2,128,128]{4,3,2,1,0:T(8,128)(2,1)S(1)}, u32[]{:S(2)}, u32[]{:S(2)}) collective-permute-start(bf16[3,2,2,128,128]{4,3,2,1,0:T(8,128)(2,1)S(1)} %collective-permute-done.3), channel_id=1, source_target_pairs={{0,32},{32,64},{64,96},{96,128},{128,160},{160,192},{192,224},{224... | collective-permute-start | bytes 1179656 | tf_op jit(solution)/shard_map/ppermute | solution.py:54
  41.6 9.8 %collective-permute-start.11 = (bf16[3,2,2,128,128]{4,3,2,1,0:T(8,128)(2,1)S(1)}, bf16[3,2,2,128,128]{4,3,2,1,0:T(8,128)(2,1)}, u32[]{:S(2)}, u32[]{:S(2)}) collective-permute-start(bf16[3,2,2,128,128]{4,3,2,1,0:T(8,128)(2,1)S(1)} %collective-permute-done.10), channel_id=1, source_target_pairs={{0,480},{32,0},{64,32},{96,64},{128,96},{160,128},{192,160},{224,1... | collective-permute-start | bytes 1179656 | tf_op jit(solution)/shard_map/ppermute | solution.py:56
  49.2 9.4 %copy-start.3 = (bf16[3,2,2,128,128]{4,3,2,1,0:T(8,128)(2,1)}, bf16[3,2,2,128,128]{4,3,2,1,0:T(8,128)(2,1)S(1)}, u32[]{:S(2)}) copy-start(bf16[3,2,2,128,128]{4,3,2,1,0:T(8,128)(2,1)S(1)} %collective-permute-done.4) | copy-start | bytes 1179652
  49.2 9.4 %collective-permute-start.5 = (bf16[3,2,2,128,128]{4,3,2,1,0:T(8,128)(2,1)S(1)}, bf16[3,2,2,128,128]{4,3,2,1,0:T(8,128)(2,1)}, u32[]{:S(2)}, u32[]{:S(2)}) collective-permute-start(bf16[3,2,2,128,128]{4,3,2,1,0:T(8,128)(2,1)S(1)} %collective-permute-done.4), channel_id=1, source_target_pairs={{0,32},{32,64},{64,96},{96,128},{128,160},{160,192},{192,224},{224... | collective-permute-start | bytes 1179656 | tf_op jit(solution)/shard_map/ppermute | solution.py:54
  51.4 13.6 %collective-permute-start.12 = (bf16[3,2,2,128,128]{4,3,2,1,0:T(8,128)(2,1)}, bf16[3,2,2,128,128]{4,3,2,1,0:T(8,128)(2,1)}, u32[]{:S(2)}, u32[]{:S(2)}) collective-permute-start(bf16[3,2,2,128,128]{4,3,2,1,0:T(8,128)(2,1)} %collective-permute-done.11), channel_id=1, source_target_pairs={{0,480},{32,0},{64,32},{96,64},{128,96},{160,128},{192,160},{224,1... | collective-permute-start | bytes 1179656 | tf_op jit(solution)/shard_map/ppermute | solution.py:56
  58.6 12.6 %collective-permute-start.6 = (bf16[3,2,2,128,128]{4,3,2,1,0:T(8,128)(2,1)}, bf16[3,2,2,128,128]{4,3,2,1,0:T(8,128)(2,1)}, u32[]{:S(2)}, u32[]{:S(2)}) collective-permute-start(bf16[3,2,2,128,128]{4,3,2,1,0:T(8,128)(2,1)} %collective-permute-done.5), channel_id=1, source_target_pairs={{0,32},{32,64},{64,96},{96,128},{128,160},{160,192},{192,224},{224... | collective-permute-start | bytes 1179656 | tf_op jit(solution)/shard_map/ppermute | solution.py:54
  64.3 28.6 %copy-start.4 = (bf16[3,2,2,128,128]{4,3,2,1,0:T(8,128)(2,1)S(1)}, bf16[3,2,2,128,128]{4,3,2,1,0:T(8,128)(2,1)}, u32[]{:S(2)}) copy-start(bf16[3,2,2,128,128]{4,3,2,1,0:T(8,128)(2,1)} %copy-done.3) | copy-start | bytes 1179652
  64.3 28.7 %copy-start.2 = (bf16[3,2,2,128,128]{4,3,2,1,0:T(8,128)(2,1)S(1)}, bf16[3,2,2,128,128]{4,3,2,1,0:T(8,128)(2,1)}, u32[]{:S(2)}) copy-start(bf16[3,2,2,128,128]{4,3,2,1,0:T(8,128)(2,1)} %copy-done.1) | copy-start | bytes 1179652
  64.9 11.8 %collective-permute-start.13 = (bf16[3,2,2,128,128]{4,3,2,1,0:T(8,128)(2,1)}, bf16[3,2,2,128,128]{4,3,2,1,0:T(8,128)(2,1)}, u32[]{:S(2)}, u32[]{:S(2)}) collective-permute-start(bf16[3,2,2,128,128]{4,3,2,1,0:T(8,128)(2,1)} %collective-permute-done.12), channel_id=1, source_target_pairs={{0,480},{32,0},{64,32},{96,64},{128,96},{160,128},{192,160},{224,1... | collective-permute-start | bytes 1179656 | tf_op jit(solution)/shard_map/ppermute | solution.py:56
  71.2 8.6 %collective-permute-start.7 = (bf16[3,2,2,128,128]{4,3,2,1,0:T(8,128)(2,1)}, bf16[3,2,2,128,128]{4,3,2,1,0:T(8,128)(2,1)}, u32[]{:S(2)}, u32[]{:S(2)}) collective-permute-start(bf16[3,2,2,128,128]{4,3,2,1,0:T(8,128)(2,1)} %collective-permute-done.6), channel_id=1, source_target_pairs={{0,32},{32,64},{64,96},{96,128},{128,160},{160,192},{192,224},{224... | collective-permute-start | bytes 1179656 | tf_op jit(solution)/shard_map/ppermute | solution.py:54
  76.8 12.9 %collective-permute-start.14 = (bf16[3,2,2,128,128]{4,3,2,1,0:T(8,128)(2,1)}, bf16[3,2,2,128,128]{4,3,2,1,0:T(8,128)(2,1)S(1)}, u32[]{:S(2)}, u32[]{:S(2)}) collective-permute-start(bf16[3,2,2,128,128]{4,3,2,1,0:T(8,128)(2,1)} %collective-permute-done.13), channel_id=1, source_target_pairs={{0,480},{32,0},{64,32},{96,64},{128,96},{160,128},{192,160},{224,1... | collective-permute-start | bytes 1179656 | tf_op jit(solution)/shard_map/ppermute | solution.py:56
  100.8 53.9 %copy-start.5 = (pred[512,4]{1,0:T(8,128)(4,1)S(1)}, pred[512,4]{1,0:T(8,128)(4,1)}, u32[]{:S(2)}) copy-start(pred[512,4]{1,0:T(8,128)(4,1)} %copy.14) | copy-start | bytes 6148
  130.3 35.5 %copy-start.6 = (pred[512]{0:T(512)(128)(4,1)S(1)}, pred[512]{0:T(512)(128)(4,1)}, u32[]{:S(2)}) copy-start(pred[512]{0:T(512)(128)(4,1)} %get-tuple-element.9) | copy-start | bytes 1540
Sparse Core Ops, SparseCore 0:
  10.4 110.5 all-gather.1
